TPU v7x, 128 devices: a whole 4x4x4 slice. The times are simulated.
128 devices in a mesh: src: 8 (over y_lo, x), tgt: 16 (over z, y_hi, core).
Axes of the slice: x: 4, y: 4 (y_hi: 2, y_lo: 2; y = y_hi * 2 + y_lo), z: 4, core: 2. Of those that a mesh axis runs over, the one named last changes fastest.
Arguments:
- residual: bfloat16 [4, 512, 2304], replicated, may hold values from -6 to 6
- targets: bfloat16 [4, 2304, 512], P(None, 'tgt'), may hold values from -6 to 6
- enc_weight: bfloat16 [4, 2304, 16384], P(None, None, ('src', 'tgt')), may hold values from -0.125 to 0.125
- enc_bias: float32 [4, 16384], P(None, ('src', 'tgt')), may hold values from -3 to 3
- active: int32 [4, 512, 16384], P(None, None, ('src', 'tgt')), may hold values 0 or 1
- dec_weight: bfloat16 [80, 2304, 2048], P('src', 'tgt'), may hold values from -0.046875 to 0.046875
- dec_bias: float32 [4, 2304], P(None, 'tgt'), may hold values from -3 to 3
- tile_pairs: int32 [80, 2], P('src'), may hold values from 0 to 3, as said below
Outputs:
- dec_grad: bfloat16 [80, 2304, 2048], P('src', 'tgt')
- enc_grad: bfloat16 [4, 2304, 16384], P(None, None, ('src', 'tgt'))
- bias_grad: float32 [4, 16384], P(None, ('src', 'tgt'))
Inputs may be any that keep to these rules, and one draw needn't show every extreme that they name: `tile_pairs`: rows b * 10 to (b + 1) * 10 - 1 serve latent block b; among them each pair (source, target) with source <= target appears exactly once, source in column 0 and target in column 1.
All inputs are finite; a program needn't handle non-finite values. No bound on the sum of `active` on one device may be relied on, other than what follows from the above.
Results may differ from a plain program's by a relative error of at most 0.019.
Values may be sent and summed in bfloat16 or wider, within the bound.
A program may use at most 128 MiB of HBM per device.

v0:
```python
import jax
import jax.numpy as jnp
from jax import lax
from jax.sharding import PartitionSpec as P


def select_layer(array, index):
    return lax.dynamic_index_in_dim(array, index, 0, keepdims=False)


def add_layer(total, index, value):
    current = lax.dynamic_slice_in_dim(total, index, 1, 0)
    return lax.dynamic_update_slice_in_dim(total, current + value[None], index, 0)


def decoder_term(error_rows, lat_block):
    product = lax.dot_general(
        error_rows, lat_block, (((1,), (0,)), ((), ())), preferred_element_type=jnp.float32
    )
    return product.astype(jnp.bfloat16)


def shards(residual, targets, enc_weight, enc_bias, active, dec_weight, dec_bias, tile_pairs):
    layers = residual.shape[0]
    tok_all = residual.shape[1]
    width_part = targets.shape[1]
    block_width = dec_weight.shape[2]
    mask_own = active.astype(jnp.float32)
    preact = jnp.einsum("lrd,ldc->lrc", residual, enc_weight, preferred_element_type=jnp.float32)
    latent = ((preact + enc_bias[:, None, :]) * mask_own).astype(jnp.bfloat16)
    blocks = lax.all_gather(latent, "tgt", axis=2, tiled=True)
    source_ids = tile_pairs[:, 0]
    target_ids = tile_pairs[:, 1]

    def add_recon(recon_sum, slot_data):
        weight, source, target = slot_data
        lat_block = select_layer(blocks, source)
        recon_term = lax.dot_general(
            weight, lat_block, (((1,), (1,)), ((), ())), preferred_element_type=jnp.float32
        )
        return (add_layer(recon_sum, target, recon_term), None)

    recon_zero = jnp.zeros((layers, width_part, tok_all), jnp.float32)
    recon_sum = lax.scan(add_recon, recon_zero, (dec_weight, source_ids, target_ids))[0]
    whole_sum = lax.psum(recon_sum.astype(jnp.bfloat16), "src").astype(jnp.float32)
    error_part = (whole_sum + dec_bias[:, :, None] - targets.astype(jnp.float32)).astype(
        jnp.bfloat16
    )

    def step_partial(grad_sum, slot_data):
        weight, source, target = slot_data
        error_rows = select_layer(error_part, target)
        lat_block = select_layer(blocks, source)
        lat_term = lax.dot_general(
            error_rows, weight, (((0,), (0,)), ((), ())), preferred_element_type=jnp.float32
        )
        return (add_layer(grad_sum, source, lat_term), decoder_term(error_rows, lat_block))

    grad_zero = jnp.zeros((layers, tok_all, block_width), jnp.float32)
    grad_sum, dec_grad = lax.scan(step_partial, grad_zero, (dec_weight, source_ids, target_ids))
    owned_grad = lax.psum_scatter(
        grad_sum.astype(jnp.bfloat16), "tgt", scatter_dimension=2, tiled=True
    ).astype(jnp.float32)
    pre_grad = (owned_grad * mask_own).astype(jnp.bfloat16)
    enc_grad = jnp.einsum(
        "lrd,lrc->ldc", residual, pre_grad, preferred_element_type=jnp.float32
    ).astype(jnp.bfloat16)
    bias_grad = jnp.sum(pre_grad.astype(jnp.float32), axis=1)
    return (dec_grad, enc_grad, bias_grad)


def solution(mesh):
    in_specs = (
        P(),
        P(None, "tgt", None),
        P(None, None, ("src", "tgt")),
        P(None, ("src", "tgt")),
        P(None, None, ("src", "tgt")),
        P("src", "tgt", None),
        P(None, "tgt"),
        P("src", None),
    )
    out_specs = (P("src", "tgt", None), P(None, None, ("src", "tgt")), P(None, ("src", "tgt")))
    return jax.shard_map(shards, mesh=mesh, in_specs=in_specs, out_specs=out_specs, check_vma=False)
```

profile of v0, /device:TPU:0, one launch (start us, length us, event | category | flops | bytes accessed | tf_op | source)
XLA Modules:
  0.0 544.1 jit_solution(14176928572429023302)
XLA Ops:
  7.2 1.6 copy-done
  8.8 7.4 %fusion.30 = bf16[4,512,128]{2,1,0:T(8,128)(2,1)} fusion(bf16[4,512,2304]{2,1,0:T(8,128)(2,1)} %param.12, bf16[4,2304,128]{2,1,0:T(8,128)(2,1)S(1)} %copy-done, s32[4,512,128]{2,1,0:T(8,128)} %param.16, f32[4,128]{1,0:T(4,128)} %param.15), kind=kOutput, calls=%fused_computation.28 | convolution fusion | flops 1209008128 | bytes 13371392 | tf_op jit(solution)/shard_map/lrd,ldc->lrc/dot_general | solution.py:29
  16.4 79.1 %all-gather.2.cloned.1.call-done = bf16[4,512,2048]{2,1,0:T(8,128)(2,1)} async-done(((bf16[4,512,128]{2,1,0:T(8,128)(2,1)}), bf16[4,512,2048]{2,1,0:T(8,128)(2,1)}) %all-gather.2.cloned.1.call-update) | async-done | bytes 8388624 | tf_op jit(solution)/shard_map/all_gather | solution.py:31
  95.7 77.2 %while.22 = (s32[]{:T(128)}, f32[4,144,512]{2,1,0:T(8,128)S(1)}, s32[10]{0:T(128)S(1)}, bf16[10,144,2048]{2,1,0:T(8,128)(2,1)}, s32[10]{0:T(128)S(1)}, /*index=5...) while((s32[]{:T(128)}, f32[4,144,512]{2,1,0:T(8,128)S(1)}, s32[10]{0:T(128)S(1)}, ...), condition=%wide.region_1.2_spmd, body=%wide.region_0.1_spmd.sunk | while | flops 302063616 | bytes 3277005 | solution.py:44
  98.2 0.6 dynamic_slice.85
  100.8 2.6 fusion.45
  105.9 0.6 dynamic_slice.85
  108.5 2.6 fusion.45
  113.7 0.6 dynamic_slice.85
  116.2 2.6 fusion.45
  121.4 0.6 dynamic_slice.85
  123.9 2.6 fusion.45
  129.1 0.6 dynamic_slice.85
  131.6 2.6 fusion.45
  136.8 0.6 dynamic_slice.85
  139.3 2.6 fusion.45
  144.5 0.6 dynamic_slice.85
  147.1 2.6 fusion.45
  152.3 0.6 dynamic_slice.85
  154.8 2.6 fusion.45
  160.0 0.6 dynamic_slice.85
  162.5 2.6 fusion.45
  167.7 0.6 dynamic_slice.85
  170.2 2.6 fusion.45
  172.9 0.9 convert_element_type.41
  174.0 72.7 %all-reduce.2.cloned.1.call-done = bf16[4,144,512]{2,1,0:T(8,128)(2,1)} async-done(((bf16[4,144,512]{2,1,0:T(8,128)(2,1)}), bf16[4,144,512]{2,1,0:T(8,128)(2,1)}) %all-reduce.2.cloned.1.call-update) | async-done | bytes 589840 | tf_op jit(solution)/shard_map/psum | solution.py:45
  246.8 1.3 subtract_convert_fusion
  248.1 7.9 %broadcast_in_dim.21 = f32[4,512,2048]{2,1,0:T(8,128)} broadcast(f32[]{:T(128)} %constant.31.clone.1), dimensions={} | broadcast | bytes 16777220 | tf_op jit(solution)/shard_map/broadcast_in_dim | solution.py:59
  255.9 130.4 %while.23 = (s32[]{:T(128)}, f32[4,512,2048]{2,1,0:T(8,128)}, bf16[10,144,2048]{2,1,0:T(8,128)(2,1)}, s32[10]{0:T(128)S(1)}, s32[10]{0:T(128)S(1)}, /*index=5*/b...) while((s32[]{:T(128)}, f32[4,512,2048]{2,1,0:T(8,128)}, ...), condition=%wide.region_4.5_spmd, body=%wide.region_3.4_spmd.sunk | while | flops 605323264 | bytes 11960553 | solution.py:60
  258.5 0.6 dynamic_slice.92
  261.0 2.9 fusion.51
  263.9 5.1 fusion.50
  271.5 0.6 dynamic_slice.92
  274.0 2.9 fusion.51
  276.9 5.1 fusion.50
  284.5 0.6 dynamic_slice.92
  287.0 2.9 fusion.51
  289.9 5.1 fusion.50
  297.6 0.6 dynamic_slice.92
  300.1 2.9 fusion.51
  303.0 5.1 fusion.50
  310.6 0.6 dynamic_slice.92
  313.1 2.9 fusion.51
  316.0 5.1 fusion.50
  323.7 0.6 dynamic_slice.92
  326.2 2.9 fusion.51
  329.1 5.1 fusion.50
  339.2 2.9 fusion.51
  342.1 5.1 fusion.50
  349.7 0.6 dynamic_slice.92
  352.2 2.9 fusion.51
  355.1 5.1 fusion.50
  365.3 2.9 fusion.51
  368.2 5.1 fusion.50
  378.4 2.9 fusion.51
  381.3 5.1 fusion.50
  386.3 9.1 %convert_element_type.45 = bf16[4,512,2048]{2,1,0:T(8,128)(2,1)} convert(f32[4,512,2048]{2,1,0:T(8,128)} %get-tuple-element.80) | non-fusion elementwise | flops 4194304 | bytes 25165824 | tf_op jit(solution)/shard_map/convert_element_type | solution.py:62
  395.4 14.6 %copy.16 = bf16[4,512,2048]{1,0,2:T(4,128)(2,1)} copy(bf16[4,512,2048]{2,1,0:T(8,128)(2,1)} %convert_element_type.45) | data formatting | bytes 16777216
  410.0 10.2 %copy.18 = bf16[256,8,4,512]{3,1,2,0:T(8,128)(2,1)} copy(bf16[256,8,4,512]{3,2,1,0:T(4,128)(2,1)} %bitcast.81) | data formatting | bytes 16777216
  420.3 102.1 %reduce-scatter.4.cloned.1.call-done = bf16[128,2048]{1,0:T(8,128)(2,1)} async-done(((bf16[2048,2048]{1,0:T(8,128)(2,1)}), bf16[128,2048]{1,0:T(8,128)(2,1)}) %reduce-scatter.4.cloned.1.call-update) | async-done | bytes 524304
  522.4 1.4 reshape.9
  524.3 2.1 convert_reduce_fusion
  526.4 6.9 %fusion.28 = bf16[4,2304,128]{1,2,0:T(8,128)(2,1)} fusion(bf16[4,512,2304]{2,1,0:T(8,128)(2,1)} %param.12, bf16[4,512,128]{2,1,0:T(8,128)(2,1)S(1)} %copy.17, s32[4,512,128]{2,1,0:T(8,128)} %param.16), kind=kOutput, calls=%fused_computation.25 | convolution fusion | flops 1210187776 | bytes 13369344 | tf_op jit(solution)/shard_map/lrd,lrc->ldc/dot_general | solution.py:65
  533.3 4.3 copy.14
  (42 shorter events, 14.4 us)
Async XLA Ops:
  7.2 1.7 copy-start
  7.2 9.2 %copy-start.4 = (s32[10,2]{0,1:T(2,128)S(1)}, s32[10,2]{0,1:T(2,128)}, u32[]{:S(2)}) copy-start(s32[10,2]{0,1:T(2,128)} %param.19) | copy-start | bytes 244
  7.2 88.3 %all-gather.2.cloned.1.call-start = ((), (), s32[]{:S(2)}) async-start(), calls=%async_computation.1 | async-start | bytes 8912896 | tf_op jit(solution)/shard_map/all_gather | solution.py:31
  16.3 230.4 %all-reduce.2.cloned.1.call-start = ((), (), s32[]{:S(2)}) async-start(), calls=%async_computation.2 | async-start | bytes 1179648 | tf_op jit(solution)/shard_map/psum | solution.py:45
  95.7 151.1 %copy-start.2 = (bf16[4,144,512]{2,1,0:T(8,128)(2,1)S(1)}, bf16[4,144,512]{2,1,0:T(8,128)(2,1)}, u32[]{:S(2)}) copy-start(bf16[4,144,512]{2,1,0:T(8,128)(2,1)} %param.13) | copy-start | bytes 1769476
  95.7 151.1 %copy-start.3 = (f32[4,144]{1,0:T(4,128)S(1)}, f32[4,144]{1,0:T(4,128)}, u32[]{:S(2)}) copy-start(f32[4,144]{1,0:T(4,128)} %param.18) | copy-start | bytes 6916
  173.8 348.6 %reduce-scatter.4.cloned.1.call-start = ((), (), s32[]{:S(2)}) async-start(), calls=%async_computation.3 | async-start | bytes 8912896
  524.3 13.3 %copy-start.1 = (bf16[4,2304,128]{2,1,0:T(8,128)(2,1)S(1)}, bf16[4,2304,128]{2,1,0:T(8,128)(2,1)}, u32[]{:S(2)}) copy-start(bf16[4,2304,128]{2,1,0:T(8,128)(2,1)} %param.14) | copy-start | bytes 7077892
Sparse Core Ops, SparseCore 0:
  16.4 79.0 all-gather.1
  173.9 72.7 all-reduce.1
  420.4 101.9 reduce-scatter.3
where the time goes:
time: 547 us; the launch traced here: 544 us
  waiting for transfers between devices  254 us (46%)
  matrix products  121 us (22%)
  loops' own time  78 us (14%)
  local copies, waits for them, and re-layouts  64 us (12%)
  between operations  13.8 us (3%)
  other arithmetic  13.4 us (2%)
    unnamed x4, waiting for transfers between devices  102 us
    all_gather x1, waiting for transfers between devices, shards(): blocks = lax.all_gather(latent, 'tgt', axis=2, tiled=True)  79.1 us
    psum x1, waiting for transfers between devices, shards(): lax.psum(recon_sum.astype(jnp.bfloat16), 'src').astype(jnp.float32)  72.7 us
    dot_general x10, matrix products, step_partial(): lax.dot_general(error_rows, weight, (((0,), (0,)), ((), ())), preferred_e...  50.8 us
    another operation x1, loops' own time, shards(): lax.scan(add_recon, recon_zero, (dec_weight, source_ids, target_ids))[0]  39.1 us
    another operation x1, loops' own time, shards(): lax.scan(step_partial, grad_zero, (dec_weight, source_ids, target_ids))  38.9 us
    unnamed x15, local copies, waits for them, and re-layouts  32.6 us
    dot_general x10, matrix products, decoder_term(): lax.dot_general(error_rows, lat_block, (((1,), (0,)), ((), ())), preferre...  29 us
  transfers between devices with their start and end apart: 3, of which 3 were waited for; matrix products, arithmetic and copies ran while one was open for 0% of the time, Pallas kernels for 0%

commit v1 on v0

--- a/solution.py
+++ b/solution.py
@@ -2,6 +2,7 @@
 import jax.numpy as jnp
 from jax import lax
 from jax.sharding import PartitionSpec as P
+from jax.lax import all_to_all, axis_size
 
 
 def select_layer(array, index):
@@ -28,7 +29,10 @@
     mask_own = active.astype(jnp.float32)
     preact = jnp.einsum("lrd,ldc->lrc", residual, enc_weight, preferred_element_type=jnp.float32)
     latent = ((preact + enc_bias[:, None, :]) * mask_own).astype(jnp.bfloat16)
-    blocks = lax.all_gather(latent, "tgt", axis=2, tiled=True)
+    wide_out = jnp.stack([latent for _ in range(axis_size("tgt"))])
+    blocks = jnp.concatenate(
+        all_to_all(wide_out, axis_name="tgt", split_axis=0, concat_axis=0), axis=2
+    )
     source_ids = tile_pairs[:, 0]
     target_ids = tile_pairs[:, 1]
 

time: 547 us -> 601 us (1.099)
  local copies, waits for them, and re-layouts: 64 us -> 92.2 us
  waiting for transfers between devices: 254 us -> 272 us
  starting transfers between devices: 0.3 us -> 8.61 us
    all_to_all x0 -> x1, waiting for transfers between devices: none -> 96.7 us  [shards(): all_to_all(wide_out, axis_name='tgt', split_axis=0, concat_axis=0)]
    all_gather x1 -> x0, waiting for transfers between devices: 79.1 us -> none  [shards(): blocks = lax.all_gather(latent, 'tgt', axis=2, tiled=True)]
    while x0 -> x1, local copies, waits for them, and re-layouts: none -> 11.5 us  [shards(): lax.scan(add_recon, recon_zero, (dec_weight, source_ids, target_ids))[0]]
    all_to_all x0 -> x1, local copies, waits for them, and re-layouts: none -> 11.4 us  [shards(): all_to_all(wide_out, axis_name='tgt', split_axis=0, concat_axis=0)]
    all_to_all x0 -> x1, starting transfers between devices: none -> 8.34 us  [shards(): all_to_all(wide_out, axis_name='tgt', split_axis=0, concat_axis=0)]
    unnamed x4 -> x3, waiting for transfers between devices: 102 us -> 102 us
where the time goes in v1:
time: 601 us; the launch traced here: 598 us
  waiting for transfers between devices  272 us (45%)
  matrix products  120 us (20%)
  local copies, waits for them, and re-layouts  92.2 us (15%)
  loops' own time  78 us (13%)
  between operations  14.1 us (2%)
  other arithmetic  13.4 us (2%)
  starting transfers between devices  8.61 us (1%)
    unnamed x3, waiting for transfers between devices  102 us
    all_to_all x1, waiting for transfers between devices, shards(): all_to_all(wide_out, axis_name='tgt', split_axis=0, concat_axis=0)  96.7 us
    psum x1, waiting for transfers between devices, shards(): lax.psum(recon_sum.astype(jnp.bfloat16), 'src').astype(jnp.float32)  72.8 us
    dot_general x10, matrix products, step_partial(): lax.dot_general(error_rows, weight, (((0,), (0,)), ((), ())), preferred_e...  50.9 us
    another operation x1, loops' own time, shards(): lax.scan(add_recon, recon_zero, (dec_weight, source_ids, target_ids))[0]  39.1 us
    another operation x1, loops' own time, shards(): lax.scan(step_partial, grad_zero, (dec_weight, source_ids, target_ids))  38.9 us
    unnamed x15, local copies, waits for them, and re-layouts  32.6 us
    dot_general x10, matrix products, decoder_term(): lax.dot_general(error_rows, lat_block, (((1,), (0,)), ((), ())), preferre...  29 us
  transfers between devices with their start and end apart: 3, of which 3 were waited for; matrix products, arithmetic and copies ran while one was open for 0% of the time, Pallas kernels for 0%

profile of v1, /device:TPU:0, one launch (start us, length us, event | category | flops | bytes accessed | tf_op | source)
XLA Modules:
  0.0 597.6 jit_solution(13098670512011797560)
XLA Ops:
  7.2 1.7 copy-done
  8.8 6.6 %fusion.30 = bf16[4,512,128]{2,1,0:T(8,128)(2,1)S(1)} fusion(bf16[4,512,2304]{2,1,0:T(8,128)(2,1)} %param.12, bf16[4,2304,128]{2,1,0:T(8,128)(2,1)S(1)} %copy-done, s32[4,512,128]{2,1,0:T(8,128)} %param.16, f32[4,128]{1,0:T(4,128)} %param.15), kind=kOutput, calls=%fused_computation.28 | convolution fusion | flops 1209008128 | bytes 13371392 | tf_op jit(solution)/shard_map/lrd,ldc->lrc/dot_general | solution.py:30
  15.5 5.2 stack.2
  20.7 8.3 %all-to-all-start = ((bf16[16,4,512,128]{3,2,1,0:T(8,128)(2,1)}), bf16[16,4,512,128]{3,2,1,0:T(8,128)(2,1)}, u32[]{:S(2)}, u32[]{:S(2)}) async-start(bf16[16,4,512,128]{3,2,1,0:T(8,128)(2,1)} %stack.2), calls=%async_computation | async-start | bytes 16777216 | tf_op jit(solution)/shard_map/all_to_all | solution.py:34
  29.2 96.7 %all-to-all-done = bf16[16,4,512,128]{3,2,1,0:T(8,128)(2,1)} async-done(((bf16[16,4,512,128]{3,2,1,0:T(8,128)(2,1)}), bf16[16,4,512,128]{3,2,1,0:T(8,128)(2,1)}, u32[]{:S(2)}, u32[]{:S(2)}) %all-to-all-start) | async-done | bytes 8388640 | tf_op jit(solution)/shard_map/all_to_all | solution.py:34
  125.8 11.4 %copy.15 = bf16[16,4,512,128]{2,3,0,1:T(8,128)(2,1)} copy(bf16[16,4,512,128]{3,2,1,0:T(8,128)(2,1)} %all-to-all-done) | data formatting | bytes 16777216 | tf_op jit(solution)/shard_map/all_to_all | solution.py:34
  137.3 11.5 %copy.16 = bf16[4,512,2048]{2,1,0:T(8,128)(2,1)} copy(bf16[4,512,2048]{1,2,0:T(8,128)(2,1)} %bitcast.84) | data formatting | bytes 16777216 | tf_op jit(solution)/shard_map/while | solution.py:48
  148.9 77.2 %while.22 = (s32[]{:T(128)}, f32[4,144,512]{2,1,0:T(8,128)S(1)}, s32[10]{0:T(128)S(1)}, bf16[10,144,2048]{2,1,0:T(8,128)(2,1)}, s32[10]{0:T(128)S(1)}, /*index=5...) while((s32[]{:T(128)}, f32[4,144,512]{2,1,0:T(8,128)S(1)}, s32[10]{0:T(128)S(1)}, ...), condition=%wide.region_1.2_spmd, body=%wide.region_0.1_spmd.sunk | while | flops 302063616 | bytes 3277005 | solution.py:48
  151.4 0.6 dynamic_slice.85
  154.0 2.6 fusion.45
  159.1 0.6 dynamic_slice.85
  161.7 2.6 fusion.45
  169.4 2.6 fusion.45
  177.1 2.6 fusion.45
  184.8 2.6 fusion.45
  192.6 2.6 fusion.45
  200.3 2.6 fusion.45
  208.0 2.6 fusion.45
  215.7 2.6 fusion.45
  220.9 0.6 dynamic_slice.85
  223.4 2.6 fusion.45
  226.1 0.9 convert_element_type.41
  227.2 72.8 %all-reduce.2.cloned.1.call-done = bf16[4,144,512]{2,1,0:T(8,128)(2,1)} async-done(((bf16[4,144,512]{2,1,0:T(8,128)(2,1)}), bf16[4,144,512]{2,1,0:T(8,128)(2,1)}) %all-reduce.2.cloned.1.call-update) | async-done | bytes 589840 | tf_op jit(solution)/shard_map/psum | solution.py:49
  300.1 1.3 subtract_convert_fusion
  301.4 7.9 %broadcast_in_dim.21 = f32[4,512,2048]{2,1,0:T(8,128)} broadcast(f32[]{:T(128)} %constant.31.clone.1), dimensions={} | broadcast | bytes 16777220 | tf_op jit(solution)/shard_map/broadcast_in_dim | solution.py:63
  309.2 130.5 %while.23 = (s32[]{:T(128)}, f32[4,512,2048]{2,1,0:T(8,128)}, bf16[10,144,2048]{2,1,0:T(8,128)(2,1)}, s32[10]{0:T(128)S(1)}, s32[10]{0:T(128)S(1)}, /*index=5*/b...) while((s32[]{:T(128)}, f32[4,512,2048]{2,1,0:T(8,128)}, ...), condition=%wide.region_4.5_spmd, body=%wide.region_3.4_spmd.sunk | while | flops 605323264 | bytes 11960553 | solution.py:64
  311.8 0.6 dynamic_slice.92
  314.3 2.9 fusion.51
  317.2 5.1 fusion.50
  324.8 0.6 dynamic_slice.92
  327.3 2.9 fusion.51
  330.2 5.1 fusion.50
  337.8 0.6 dynamic_slice.92
  340.3 2.9 fusion.51
  343.2 5.1 fusion.50
  350.9 0.6 dynamic_slice.92
  353.4 2.9 fusion.51
  356.3 5.1 fusion.50
  363.9 0.6 dynamic_slice.92
  366.4 2.9 fusion.51
  369.3 5.1 fusion.50
  377.0 0.6 dynamic_slice.92
  379.5 2.9 fusion.51
  382.4 5.1 fusion.50
  390.0 0.6 dynamic_slice.92
  392.5 2.9 fusion.51
  395.4 5.1 fusion.50
  403.0 0.6 dynamic_slice.92
  405.6 2.9 fusion.51
  408.5 5.1 fusion.50
  416.1 0.6 dynamic_slice.92
  418.6 2.9 fusion.51
  421.5 5.1 fusion.50
  429.2 0.6 dynamic_slice.92
  431.7 2.9 fusion.51
  434.6 5.1 fusion.50
  439.7 9.1 %convert_element_type.45 = bf16[4,512,2048]{2,1,0:T(8,128)(2,1)} convert(f32[4,512,2048]{2,1,0:T(8,128)} %get-tuple-element.80) | non-fusion elementwise | flops 4194304 | bytes 25165824 | tf_op jit(solution)/shard_map/convert_element_type | solution.py:66
  448.8 14.5 %copy.21 = bf16[4,512,2048]{1,0,2:T(4,128)(2,1)} copy(bf16[4,512,2048]{2,1,0:T(8,128)(2,1)} %convert_element_type.45) | data formatting | bytes 16777216
  463.3 10.2 %copy.23 = bf16[256,8,4,512]{3,1,2,0:T(8,128)(2,1)} copy(bf16[256,8,4,512]{3,2,1,0:T(4,128)(2,1)} %bitcast.85) | data formatting | bytes 16777216
  473.6 102.1 %reduce-scatter.4.cloned.1.call-done = bf16[128,2048]{1,0:T(8,128)(2,1)} async-done(((bf16[2048,2048]{1,0:T(8,128)(2,1)}), bf16[128,2048]{1,0:T(8,128)(2,1)}) %reduce-scatter.4.cloned.1.call-update) | async-done | bytes 524304
  575.7 1.4 reshape.19
  577.5 2.1 convert_reduce_fusion
  579.6 6.9 %fusion.28 = bf16[4,2304,128]{1,2,0:T(8,128)(2,1)} fusion(bf16[4,512,2304]{2,1,0:T(8,128)(2,1)} %param.12, bf16[4,512,128]{2,1,0:T(8,128)(2,1)S(1)} %copy.22, s32[4,512,128]{2,1,0:T(8,128)} %param.16), kind=kOutput, calls=%fused_computation.25 | convolution fusion | flops 1210187776 | bytes 13369344 | tf_op jit(solution)/shard_map/lrd,lrc->ldc/dot_general | solution.py:69
  586.5 4.3 copy.19
  (44 shorter events, 16.7 us)
Async XLA Ops:
  7.2 1.7 copy-start
  20.7 8.4 %copy-start.4 = (s32[10,2]{0,1:T(2,128)S(1)}, s32[10,2]{0,1:T(2,128)}, u32[]{:S(2)}) copy-start(s32[10,2]{0,1:T(2,128)} %param.19) | copy-start | bytes 244
  20.7 105.1 %all-to-all-start = ((bf16[16,4,512,128]{3,2,1,0:T(8,128)(2,1)}), bf16[16,4,512,128]{3,2,1,0:T(8,128)(2,1)}, u32[]{:S(2)}, u32[]{:S(2)}) async-start(bf16[16,4,512,128]{3,2,1,0:T(8,128)(2,1)} %stack.2), calls=%async_computation | async-start | bytes 16777216 | tf_op jit(solution)/shard_map/all_to_all | solution.py:34
  29.1 271.0 %all-reduce.2.cloned.1.call-start = ((), (), s32[]{:S(2)}) async-start(), calls=%async_computation.2 | async-start | bytes 1179648 | tf_op jit(solution)/shard_map/psum | solution.py:49
  148.9 151.2 %copy-start.2 = (bf16[4,144,512]{2,1,0:T(8,128)(2,1)S(1)}, bf16[4,144,512]{2,1,0:T(8,128)(2,1)}, u32[]{:S(2)}) copy-start(bf16[4,144,512]{2,1,0:T(8,128)(2,1)} %param.13) | copy-start | bytes 1769476
  148.9 151.2 %copy-start.3 = (f32[4,144]{1,0:T(4,128)S(1)}, f32[4,144]{1,0:T(4,128)}, u32[]{:S(2)}) copy-start(f32[4,144]{1,0:T(4,128)} %param.18) | copy-start | bytes 6916
  227.0 348.7 %reduce-scatter.4.cloned.1.call-start = ((), (), s32[]{:S(2)}) async-start(), calls=%async_computation.3 | async-start | bytes 8912896
  577.5 13.3 %copy-start.1 = (bf16[4,2304,128]{2,1,0:T(8,128)(2,1)S(1)}, bf16[4,2304,128]{2,1,0:T(8,128)(2,1)}, u32[]{:S(2)}) copy-start(bf16[4,2304,128]{2,1,0:T(8,128)(2,1)} %param.14) | copy-start | bytes 7077892
Sparse Core Ops, SparseCore 0:
  227.1 72.8 all-reduce.1
  473.7 101.9 reduce-scatter.3
